TPU v7x, 128 devices: a whole 4x4x4 slice. The times are simulated.
128 devices in a mesh: dp: 32 (over z, x, core), seq: 4 (over y).
Axes of the slice: x: 4, y: 4, z: 4, core: 2. Of those that a mesh axis runs over, the one named last changes fastest.
Arguments:
- queries: bfloat16 [32768, 2560], P(('dp', 'seq')), may hold values from -200 to 200
- keys: bfloat16 [32768, 2560], P(('dp', 'seq')), may hold values from -200 to 200
- values: bfloat16 [32768, 2560], P(('dp', 'seq')), may hold values from -6 to 6
- gain_q: float32 [2560], replicated, may hold values from 0.5 to 1.5
- gain_k: float32 [2560], replicated, may hold values from 0.5 to 1.5
- tile_pairs: int32 [16, 8], replicated, may hold values from 0 to 15, as said below
- tile_lens: int32 [32, 16], P('dp'), may hold values from 40 to 64
- out_grad: bfloat16 [32768, 5120], P(('dp', 'seq')), may hold values from -24 to 24
- w_out: bfloat16 [5120, 2560], P('dp', 'seq'), may hold values from -0.125 to 0.125
Outputs:
- grad_q: bfloat16 [32768, 2560], P(('dp', 'seq'))
- grad_k: bfloat16 [32768, 2560], P(('dp', 'seq'))
- grad_v: bfloat16 [32768, 2560], P(('dp', 'seq'))
- grad_w: float32 [5120, 2560], P('dp', 'seq')
Inputs may be any that keep to these rules, and one draw needn't show every extreme that they name: `tile_pairs`: row a lists 8 different tiles of the window, with tile a first.
All inputs are finite; a program needn't handle non-finite values.
Results may differ from a plain program's by a relative error of at most 0.02.
Values may be sent and summed in bfloat16 or wider, within the bound.
No kernel may reach another device: no remote copies, remote signals or barrier semaphores. Data moves between devices by JAX's collectives and lax.ppermute only.
A program may use at most 128 MiB of HBM per device.

v0:
```python
import math
import jax
import jax.numpy as jnp
from jax import lax
from jax.sharding import PartitionSpec as P

HEAD_DIM = 128
EPS = 1e-06


def multiply(pattern, left, right):
    return jnp.einsum(pattern, left, right, preferred_element_type=jnp.float32)


def normalize(field, gain):
    values_f = field.astype(jnp.float32)
    row_scale = lax.rsqrt(jnp.mean(values_f * values_f, axis=-1, keepdims=True) + EPS)
    return ((values_f * row_scale * gain).astype(jnp.bfloat16), row_scale)


def norm_finish(values_f, row_scale, gated, inner, width):
    return (row_scale * gated - values_f * row_scale**3 * inner / width).astype(jnp.bfloat16)


def tile_attention(query_tiles, key_tiles, value_tiles, grad_tiles, tile_pairs, live_lengths):
    tile_count, tile_rows, head_width = query_tiles.shape
    neighbours = tile_pairs.shape[1]
    factor = 1.0 / math.sqrt(head_width)
    key_near = jnp.take(key_tiles, tile_pairs, axis=0).reshape(
        tile_count, neighbours * tile_rows, head_width
    )
    value_near = jnp.take(value_tiles, tile_pairs, axis=0).reshape(
        tile_count, neighbours * tile_rows, head_width
    )
    near_lengths = jnp.take(live_lengths, tile_pairs, axis=0)
    live = (
        jnp.arange(tile_rows, dtype=jnp.int32)[None, None, :] < near_lengths[:, :, None]
    ).reshape(tile_count, neighbours * tile_rows)
    scores = multiply("aqd,akd->aqk", query_tiles, key_near) * factor
    scores = jnp.where(live[:, None, :], scores, -jnp.inf)
    row_max = jnp.max(scores, axis=-1, keepdims=True)
    weights = jnp.exp(scores - row_max)
    probs = weights / jnp.sum(weights, axis=-1, keepdims=True)
    probs_low = probs.astype(jnp.bfloat16)
    attended = multiply("aqk,akd->aqd", probs_low, value_near).astype(jnp.bfloat16)
    grad_probs = multiply("aqd,akd->aqk", grad_tiles, value_near)
    delta = jnp.sum(probs * grad_probs, axis=-1, keepdims=True)
    grad_scores = (probs * (grad_probs - delta)).astype(jnp.bfloat16)
    grad_query = (multiply("aqk,akd->aqd", grad_scores, key_near) * factor).astype(jnp.bfloat16)
    grad_key_near = multiply("aqk,aqd->akd", grad_scores, query_tiles) * factor
    grad_value_near = multiply("aqk,aqd->akd", probs_low, grad_tiles)
    owners = (
        tile_pairs[:, :, None] == jnp.arange(tile_count, dtype=jnp.int32)[None, None, :]
    ).astype(jnp.float32)
    grad_key = jnp.einsum(
        "anb,antd->btd",
        owners,
        grad_key_near.reshape(tile_count, neighbours, tile_rows, head_width),
        precision=lax.Precision.HIGHEST,
    ).astype(jnp.bfloat16)
    grad_value = jnp.einsum(
        "anb,antd->btd",
        owners,
        grad_value_near.reshape(tile_count, neighbours, tile_rows, head_width),
        precision=lax.Precision.HIGHEST,
    ).astype(jnp.bfloat16)
    return (attended, grad_query, grad_key, grad_value)


def per_device(queries, keys, values, gain_q, gain_k, tile_pairs, tile_lens, out_grad, w_out):
    seq_count = lax.axis_size("seq")
    dp_count = lax.axis_size("dp")
    tok_rows = queries.shape[0]
    width = queries.shape[1]
    local_width = width // seq_count
    clip_rows = tok_rows * seq_count
    tile_count = tile_pairs.shape[0]
    tile_rows = clip_rows // tile_count
    head_count = local_width // HEAD_DIM
    clip_lengths = tile_lens[0]
    query_normed, query_scale = normalize(queries, gain_q)
    key_normed, key_scale = normalize(keys, gain_k)
    query_heads, key_heads, value_heads = (
        lax.all_to_all(query_normed, "seq", split_axis=1, concat_axis=0, tiled=True),
        lax.all_to_all(key_normed, "seq", split_axis=1, concat_axis=0, tiled=True),
        lax.all_to_all(values, "seq", split_axis=1, concat_axis=0, tiled=True),
    )
    cot_all = lax.all_gather(out_grad, "seq", axis=0, tiled=True)
    columns = cot_all
    grad_attended = jnp.dot(
        columns, lax.all_gather(w_out, "dp", axis=0, tiled=True), preferred_element_type=jnp.float32
    ).astype(jnp.bfloat16)

    def split(field):
        return field.reshape(tile_count, tile_rows, head_count, HEAD_DIM).transpose(2, 0, 1, 3)

    def merge(field):
        return field.transpose(1, 2, 0, 3).reshape(clip_rows, local_width)

    def one_head(group):
        return tile_attention(group[0], group[1], group[2], group[3], tile_pairs, clip_lengths)

    attended, grad_qn, grad_kn, grad_vh = lax.map(
        one_head, (split(query_heads), split(key_heads), split(value_heads), split(grad_attended))
    )
    attended = merge(attended)
    grad_qn = merge(grad_qn)
    grad_kn = merge(grad_kn)
    grad_vh = merge(grad_vh)
    columns = cot_all
    grad_w = lax.psum_scatter(
        (
            jnp.einsum("td,te->de", columns, attended, preferred_element_type=jnp.float32)
            / dp_count
        ).astype(jnp.bfloat16),
        "dp",
        scatter_dimension=0,
        tiled=True,
    ).astype(jnp.float32)
    grad_qt, grad_kt, grad_v = (
        lax.all_to_all(grad_qn, "seq", split_axis=0, concat_axis=1, tiled=True),
        lax.all_to_all(grad_kn, "seq", split_axis=0, concat_axis=1, tiled=True),
        lax.all_to_all(grad_vh, "seq", split_axis=0, concat_axis=1, tiled=True),
    )
    query_full = queries.astype(jnp.float32)
    key_full = keys.astype(jnp.float32)
    gated_q = gain_q * grad_qt.astype(jnp.float32)
    gated_k = gain_k * grad_kt.astype(jnp.float32)
    inner_q = jnp.sum(gated_q * query_full, axis=-1, keepdims=True)
    inner_k = jnp.sum(gated_k * key_full, axis=-1, keepdims=True)
    grad_q = norm_finish(query_full, query_scale, gated_q, inner_q, width)
    grad_k = norm_finish(key_full, key_scale, gated_k, inner_k, width)
    return (grad_q, grad_k, grad_v, grad_w)


def solution(mesh):
    return jax.shard_map(
        per_device,
        mesh=mesh,
        in_specs=(
            P(("dp", "seq"), None),
            P(("dp", "seq"), None),
            P(("dp", "seq"), None),
            P(),
            P(),
            P(),
            P("dp", None),
            P(("dp", "seq"), None),
            P("dp", "seq"),
        ),
        out_specs=(
            P(("dp", "seq"), None),
            P(("dp", "seq"), None),
            P(("dp", "seq"), None),
            P("dp", "seq"),
        ),
        check_vma=False,
    )
```

profile of v0, /device:TPU:0, one launch (start us, length us, event | category | flops | bytes accessed | tf_op | source)
XLA Modules:
  0.0 484.7 jit_solution(18076181013758219229)
XLA Ops:
  12.3 4.5 all-to-all-start
  23.3 11.4 %all-to-all-done = bf16[256,4,640]{2,0,1:T(8,128)(2,1)S(1)} async-done(((bf16[256,4,640]{2,0,1:T(8,128)(2,1)}), bf16[256,4,640]{2,0,1:T(8,128)(2,1)S(1)}, u32[]{:S(2)}, u32[]{:S(2)}) %all-to-all-start) | async-done | bytes 1310752 | tf_op jit(solution)/shard_map/all_to_all | solution.py:84
  34.7 3.5 all-to-all-start.1
  40.8 14.4 %all-to-all-done.1 = bf16[256,4,640]{2,0,1:T(8,128)(2,1)S(1)} async-done(((bf16[256,4,640]{2,0,1:T(8,128)(2,1)}), bf16[256,4,640]{2,0,1:T(8,128)(2,1)S(1)}, u32[]{:S(2)}, u32[]{:S(2)}) %all-to-all-start.1) | async-done | bytes 1310752 | tf_op jit(solution)/shard_map/all_to_all | solution.py:85
  55.2 4.3 all-to-all-start.2
  63.1 3.1 reshape.159
  67.6 8.1 %all-to-all-done.2 = bf16[256,4,640]{2,0,1:T(8,128)(2,1)} async-done(((bf16[256,4,640]{2,0,1:T(8,128)(2,1)}), bf16[256,4,640]{2,0,1:T(8,128)(2,1)}, u32[]{:S(2)}, u32[]{:S(2)}) %all-to-all-start.2) | async-done | bytes 1310752 | tf_op jit(solution)/shard_map/all_to_all | solution.py:86
  75.7 3.2 reshape.160
  80.3 83.5 %all-gather.3.cloned.1.call-done = bf16[1024,5120]{1,0:T(8,128)(2,1)} async-done(((bf16[256,5120]{1,0:T(8,128)(2,1)}), bf16[1024,5120]{1,0:T(8,128)(2,1)}) %all-gather.3.cloned.1.call-update) | async-done | bytes 10485776 | tf_op jit(solution)/shard_map/all_gather | solution.py:88
  163.8 13.7 %convolution_convert_fusion.1 = bf16[1024,640]{1,0:T(8,128)(2,1)} fusion(bf16[1024,5120]{1,0:T(8,128)(2,1)} %all-gather.3.cloned.1.call-done, bf16[5120,640]{1,0:T(8,128)(2,1)} %all-gather.5.cloned.1.call-done), kind=kOutput, calls=%fused_computation.95 | convolution fusion | flops 6711541760 | bytes 18350080 | tf_op jit(solution)/shard_map/dot_general | solution.py:90
  177.5 3.1 reshape.161
  182.1 182.6 %while.18 = (s32[]{:T(128)}, bf16[5,16,64,128]{3,2,1,0:T(8,128)(2,1)}, bf16[5,16,64,128]{3,2,1,0:T(8,128)(2,1)}, bf16[5,16,64,128]{3,1,2,0:T(8,128)(2,1)}, bf16[...) while((s32[]{:T(128)}, ...), condition=%wide.region_6.8_spmd, body=%wide.region_2.7_spmd.sunk | while | flops 1219638656 | bytes 88276472 | solution.py:103
  187.9 4.0 broadcast_select_fusion.6
  194.5 3.6 fusion.136
  201.7 2.8 convolution_multiply_fusion.3
  204.6 7.3 %fusion.138 = bf16[5,16,64,128]{3,1,2,0:T(8,128)(2,1)} fusion(bf16[5,16,64,128]{3,1,2,0:T(8,128)(2,1)} %get-tuple-element.341, s32[]{:T(128)S(6)} %copy.142, f32[16,8,64,128]{3,2,1,0:T(8,128)} %bitcast.172, s32[16,8]{0,1:T(8,128)S(1)} %copy.132), kind=kOutput, calls=%fused_computation.26.clone.1 | convolution fusion | flops 201459712 | bytes 4456964 | tf_op jit(solution)/shard_map/while/body/eval_jaxpr/anb,antd->btd/dot_general | solution.py:55
  213.8 5.1 %fusion.140 = bf16[5,16,64,128]{3,1,2,0:T(8,128)(2,1)} fusion(bf16[5,16,64,128]{3,1,2,0:T(8,128)(2,1)} %get-tuple-element.342, s32[]{:T(128)S(6)} %copy.142, f32[16,8,64,128]{3,2,1,0:T(8,128)S(1)} %bitcast.177, s32[16,8]{0,1:T(8,128)S(1)} %copy.132), kind=kOutput, calls=%fused_computation.28.clone.1 | convolution fusion | flops 201459712 | bytes 4456964 | tf_op jit(solution)/shard_map/while/body/eval_jaxpr/anb,antd->btd/dot_general | solution.py:61
  224.3 4.0 broadcast_select_fusion.6
  230.9 3.6 fusion.136
  238.0 2.8 convolution_multiply_fusion.3
  240.9 7.3 %fusion.138 = bf16[5,16,64,128]{3,1,2,0:T(8,128)(2,1)} fusion(bf16[5,16,64,128]{3,1,2,0:T(8,128)(2,1)} %get-tuple-element.341, s32[]{:T(128)S(6)} %copy.142, f32[16,8,64,128]{3,2,1,0:T(8,128)} %bitcast.172, s32[16,8]{0,1:T(8,128)S(1)} %copy.132), kind=kOutput, calls=%fused_computation.26.clone.1 | convolution fusion | flops 201459712 | bytes 4456964 | tf_op jit(solution)/shard_map/while/body/eval_jaxpr/anb,antd->btd/dot_general | solution.py:55
  250.1 5.1 %fusion.140 = bf16[5,16,64,128]{3,1,2,0:T(8,128)(2,1)} fusion(bf16[5,16,64,128]{3,1,2,0:T(8,128)(2,1)} %get-tuple-element.342, s32[]{:T(128)S(6)} %copy.142, f32[16,8,64,128]{3,2,1,0:T(8,128)S(1)} %bitcast.177, s32[16,8]{0,1:T(8,128)S(1)} %copy.132), kind=kOutput, calls=%fused_computation.28.clone.1 | convolution fusion | flops 201459712 | bytes 4456964 | tf_op jit(solution)/shard_map/while/body/eval_jaxpr/anb,antd->btd/dot_general | solution.py:61
  260.7 4.0 broadcast_select_fusion.6
  267.3 3.6 fusion.136
  274.4 2.8 convolution_multiply_fusion.3
  277.3 7.2 %fusion.138 = bf16[5,16,64,128]{3,1,2,0:T(8,128)(2,1)} fusion(bf16[5,16,64,128]{3,1,2,0:T(8,128)(2,1)} %get-tuple-element.341, s32[]{:T(128)S(6)} %copy.142, f32[16,8,64,128]{3,2,1,0:T(8,128)} %bitcast.172, s32[16,8]{0,1:T(8,128)S(1)} %copy.132), kind=kOutput, calls=%fused_computation.26.clone.1 | convolution fusion | flops 201459712 | bytes 4456964 | tf_op jit(solution)/shard_map/while/body/eval_jaxpr/anb,antd->btd/dot_general | solution.py:55
  286.5 5.1 %fusion.140 = bf16[5,16,64,128]{3,1,2,0:T(8,128)(2,1)} fusion(bf16[5,16,64,128]{3,1,2,0:T(8,128)(2,1)} %get-tuple-element.342, s32[]{:T(128)S(6)} %copy.142, f32[16,8,64,128]{3,2,1,0:T(8,128)S(1)} %bitcast.177, s32[16,8]{0,1:T(8,128)S(1)} %copy.132), kind=kOutput, calls=%fused_computation.28.clone.1 | convolution fusion | flops 201459712 | bytes 4456964 | tf_op jit(solution)/shard_map/while/body/eval_jaxpr/anb,antd->btd/dot_general | solution.py:61
  297.1 4.0 broadcast_select_fusion.6
  303.6 3.6 fusion.136
  313.7 7.3 %fusion.138 = bf16[5,16,64,128]{3,1,2,0:T(8,128)(2,1)} fusion(bf16[5,16,64,128]{3,1,2,0:T(8,128)(2,1)} %get-tuple-element.341, s32[]{:T(128)S(6)} %copy.142, f32[16,8,64,128]{3,2,1,0:T(8,128)} %bitcast.172, s32[16,8]{0,1:T(8,128)S(1)} %copy.132), kind=kOutput, calls=%fused_computation.26.clone.1 | convolution fusion | flops 201459712 | bytes 4456964 | tf_op jit(solution)/shard_map/while/body/eval_jaxpr/anb,antd->btd/dot_general | solution.py:55
  322.9 5.2 %fusion.140 = bf16[5,16,64,128]{3,1,2,0:T(8,128)(2,1)} fusion(bf16[5,16,64,128]{3,1,2,0:T(8,128)(2,1)} %get-tuple-element.342, s32[]{:T(128)S(6)} %copy.142, f32[16,8,64,128]{3,2,1,0:T(8,128)S(1)} %bitcast.177, s32[16,8]{0,1:T(8,128)S(1)} %copy.132), kind=kOutput, calls=%fused_computation.28.clone.1 | convolution fusion | flops 201459712 | bytes 4456964 | tf_op jit(solution)/shard_map/while/body/eval_jaxpr/anb,antd->btd/dot_general | solution.py:61
  333.5 4.0 broadcast_select_fusion.6
  340.1 3.6 fusion.136
  350.1 7.3 %fusion.138 = bf16[5,16,64,128]{3,1,2,0:T(8,128)(2,1)} fusion(bf16[5,16,64,128]{3,1,2,0:T(8,128)(2,1)} %get-tuple-element.341, s32[]{:T(128)S(6)} %copy.142, f32[16,8,64,128]{3,2,1,0:T(8,128)} %bitcast.172, s32[16,8]{0,1:T(8,128)S(1)} %copy.132), kind=kOutput, calls=%fused_computation.26.clone.1 | convolution fusion | flops 201459712 | bytes 4456964 | tf_op jit(solution)/shard_map/while/body/eval_jaxpr/anb,antd->btd/dot_general | solution.py:55
  359.3 5.2 %fusion.140 = bf16[5,16,64,128]{3,1,2,0:T(8,128)(2,1)} fusion(bf16[5,16,64,128]{3,1,2,0:T(8,128)(2,1)} %get-tuple-element.342, s32[]{:T(128)S(6)} %copy.142, f32[16,8,64,128]{3,2,1,0:T(8,128)S(1)} %bitcast.177, s32[16,8]{0,1:T(8,128)S(1)} %copy.132), kind=kOutput, calls=%fused_computation.28.clone.1 | convolution fusion | flops 201459712 | bytes 4456964 | tf_op jit(solution)/shard_map/while/body/eval_jaxpr/anb,antd->btd/dot_general | solution.py:61
  367.0 11.5 %fusion.68 = bf16[5120,640]{0,1:T(8,128)(2,1)} fusion(bf16[1024,5120]{1,0:T(8,128)(2,1)} %all-gather.3.cloned.1.call-done, bf16[128,8,5,128]{3,2,1,0:T(8,128)(2,1)S(1)} %bitcast.191), kind=kOutput, calls=%fused_computation.66 | convolution fusion | flops 6717440000 | bytes 18350080 | tf_op jit(solution)/shard_map/td,te->de/dot_general | solution.py:113
  378.5 9.5 %copy.97 = bf16[5120,640]{1,0:T(8,128)(2,1)} copy(bf16[5120,640]{0,1:T(8,128)(2,1)} %fusion.68) | data formatting | bytes 13107200
  392.8 4.0 all-to-all-start.3
  406.2 8.4 %all-to-all-done.3 = bf16[4,256,640]{2,1,0:T(8,128)(2,1)S(1)} async-done(((bf16[4,256,640]{2,1,0:T(8,128)(2,1)}), bf16[4,256,640]{2,1,0:T(8,128)(2,1)S(1)}, u32[]{:S(2)}, u32[]{:S(2)}) %all-to-all-start.3) | async-done | bytes 1310752 | tf_op jit(solution)/shard_map/all_to_all | solution.py:121
  415.7 3.8 all-to-all-start.4
  419.5 3.1 convert_bitcast_fusion.1
  422.6 3.4 copy.85
  432.7 3.7 all-to-all-done.4
  437.5 3.5 all-to-all-start.5
  441.0 2.9 convert_bitcast_fusion
  444.0 3.4 copy.87
  454.2 2.9 all-to-all-done.5
  459.3 16.6 %reduce-scatter.4.cloned.1.call-done = bf16[160,640]{1,0:T(8,128)(2,1)} async-done(((bf16[5120,640]{1,0:T(8,128)(2,1)}), bf16[160,640]{1,0:T(8,128)(2,1)}) %reduce-scatter.4.cloned.1.call-update) | async-done | bytes 204816
  (216 shorter events, 131.2 us)
Async XLA Ops:
  7.2 52.7 %copy-start = (s32[1,16]{1,0:T(1,128)S(1)}, s32[1,16]{1,0:T(1,128)}, u32[]{:S(2)}) copy-start(s32[1,16]{1,0:T(1,128)} %param.19) | copy-start | bytes 196
  7.2 1.5 copy-start.14
  7.2 73.1 %all-gather.5.cloned.1.call-start = ((), (), s32[]{:S(2)}) async-start(), calls=%async_computation.8 | async-start | bytes 6758400 | tf_op jit(solution)/shard_map/all_gather | solution.py:91
  7.9 155.8 %all-gather.3.cloned.1.call-start = ((), (), s32[]{:S(2)}) async-start(), calls=%async_computation.7 | async-start | bytes 13107200 | tf_op jit(solution)/shard_map/all_gather | solution.py:88
  8.7 1.6 copy-start.16
  9.3 3.0 copy-start.7
  10.3 0.5 copy-start.23
  12.3 22.5 %all-to-all-start = ((bf16[256,4,640]{2,0,1:T(8,128)(2,1)}), bf16[256,4,640]{2,0,1:T(8,128)(2,1)S(1)}, u32[]{:S(2)}, u32[]{:S(2)}) async-start(bf16[256,4,640]{2,0,1:T(8,128)(2,1)} %copy.73), calls=%async_computation | async-start | bytes 2621440 | tf_op jit(solution)/shard_map/all_to_all | solution.py:84
  16.8 2.6 copy-start.18
  18.4 4.9 %copy-start.5 = (bf16[256,2560]{0,1:T(8,128)(2,1)}, bf16[256,2560]{0,1:T(8,128)(2,1)S(1)}, u32[]{:S(2)}) copy-start(bf16[256,2560]{0,1:T(8,128)(2,1)S(1)} %copy.74) | copy-start | bytes 3932164
  19.4 3.9 copy-start.21
  34.7 20.5 %all-to-all-start.1 = ((bf16[256,4,640]{2,0,1:T(8,128)(2,1)}), bf16[256,4,640]{2,0,1:T(8,128)(2,1)S(1)}, u32[]{:S(2)}, u32[]{:S(2)}) async-start(bf16[256,4,640]{2,0,1:T(8,128)(2,1)} %copy.75), calls=%async_computation.1 | async-start | bytes 2621440 | tf_op jit(solution)/shard_map/all_to_all | solution.py:85
  38.3 21.4 %copy-start.20 = (s32[16,8]{0,1:T(8,128)S(1)}, s32[16,8]{0,1:T(8,128)}, u32[]{:S(2)}) copy-start(s32[16,8]{0,1:T(8,128)} %param.18) | copy-start | bytes 1540
  55.2 5.9 %copy-start.11 = (bf16[256,4,640]{2,0,1:T(8,128)(2,1)}, bf16[256,4,640]{2,0,1:T(8,128)(2,1)S(1)}, u32[]{:S(2)}) copy-start(bf16[256,4,640]{2,0,1:T(8,128)(2,1)S(1)} %all-to-all-done.1) | copy-start | bytes 3932164
  55.2 20.5 %all-to-all-start.2 = ((bf16[256,4,640]{2,0,1:T(8,128)(2,1)}), bf16[256,4,640]{2,0,1:T(8,128)(2,1)}, u32[]{:S(2)}, u32[]{:S(2)}) async-start(bf16[256,4,640]{2,0,1:T(8,128)(2,1)} %bitcast.186), calls=%async_computation.2 | async-start | bytes 2621440 | tf_op jit(solution)/shard_map/all_to_all | solution.py:86
  59.6 416.4 %reduce-scatter.4.cloned.1.call-start = ((), (), s32[]{:S(2)}) async-start(), calls=%async_computation.9 | async-start | bytes 6758400
  194.5 3.6 copy-start.2
  194.5 3.6 copy-start.3
  204.6 7.3 %copy-start.4 = (f32[16,64,512]{2,1,0:T(8,128)S(1)}, f32[16,64,512]{2,1,0:T(8,128)}, u32[]{:S(2)}) copy-start(f32[16,64,512]{2,1,0:T(8,128)} %get-tuple-element.322) | copy-start | bytes 6291460 | tf_op jit(solution)/shard_map/while
  230.9 3.6 copy-start.2
  230.9 3.6 copy-start.3
  240.9 7.3 %copy-start.4 = (f32[16,64,512]{2,1,0:T(8,128)S(1)}, f32[16,64,512]{2,1,0:T(8,128)}, u32[]{:S(2)}) copy-start(f32[16,64,512]{2,1,0:T(8,128)} %get-tuple-element.322) | copy-start | bytes 6291460 | tf_op jit(solution)/shard_map/while
  267.3 3.6 copy-start.2
  267.3 3.6 copy-start.3
  277.3 7.3 %copy-start.4 = (f32[16,64,512]{2,1,0:T(8,128)S(1)}, f32[16,64,512]{2,1,0:T(8,128)}, u32[]{:S(2)}) copy-start(f32[16,64,512]{2,1,0:T(8,128)} %get-tuple-element.322) | copy-start | bytes 6291460 | tf_op jit(solution)/shard_map/while
  303.6 3.6 copy-start.2
  303.6 3.6 copy-start.3
  313.7 7.3 %copy-start.4 = (f32[16,64,512]{2,1,0:T(8,128)S(1)}, f32[16,64,512]{2,1,0:T(8,128)}, u32[]{:S(2)}) copy-start(f32[16,64,512]{2,1,0:T(8,128)} %get-tuple-element.322) | copy-start | bytes 6291460 | tf_op jit(solution)/shard_map/while
  340.1 3.6 copy-start.2
  340.1 3.6 copy-start.3
  350.1 7.3 %copy-start.4 = (f32[16,64,512]{2,1,0:T(8,128)S(1)}, f32[16,64,512]{2,1,0:T(8,128)}, u32[]{:S(2)}) copy-start(f32[16,64,512]{2,1,0:T(8,128)} %get-tuple-element.322) | copy-start | bytes 6291460 | tf_op jit(solution)/shard_map/while
  388.0 1.3 copy-start.15
  392.8 21.9 %all-to-all-start.3 = ((bf16[4,256,640]{2,1,0:T(8,128)(2,1)}), bf16[4,256,640]{2,1,0:T(8,128)(2,1)S(1)}, u32[]{:S(2)}, u32[]{:S(2)}) async-start(bf16[4,256,640]{2,1,0:T(8,128)(2,1)} %all_to_all.79), calls=%async_computation.3 | async-start | bytes 2621440 | tf_op jit(solution)/shard_map/all_to_all | solution.py:121
  414.7 1.1 copy-start.13
  415.7 20.7 %all-to-all-start.4 = ((bf16[4,256,640]{2,1,0:T(8,128)(2,1)}), bf16[4,256,640]{2,1,0:T(8,128)(2,1)S(1)}, u32[]{:S(2)}, u32[]{:S(2)}) async-start(bf16[4,256,640]{2,1,0:T(8,128)(2,1)} %all_to_all.81), calls=%async_computation.4 | async-start | bytes 2621440 | tf_op jit(solution)/shard_map/all_to_all | solution.py:122
  422.6 3.4 copy-start.8
  422.6 3.4 copy-start.17
  426.0 2.5 copy-start.9
  426.0 2.5 copy-start.24
  426.0 2.5 copy-start.26
  436.4 1.1 copy-start.12
  437.5 19.6 %all-to-all-start.5 = ((bf16[4,256,640]{2,1,0:T(8,128)(2,1)}), bf16[4,256,640]{2,1,0:T(8,128)(2,1)S(1)}, u32[]{:S(2)}, u32[]{:S(2)}) async-start(bf16[4,256,640]{2,1,0:T(8,128)(2,1)} %all_to_all.83), calls=%async_computation.5 | async-start | bytes 2621440 | tf_op jit(solution)/shard_map/all_to_all | solution.py:123
  444.0 3.4 copy-start.6
  444.0 3.4 copy-start.19
  447.4 2.6 copy-start.10
  447.4 2.6 copy-start.22
  447.4 2.6 copy-start.25
  457.1 20.8 %copy-start.1 = (s32[1,16]{1,0:T(1,128)S(1)}, s32[1,16]{1,0:T(1,128)}, u32[]{:S(2)}) copy-start(s32[1,16]{1,0:T(1,128)} %param.19) | copy-start | bytes 196
Sparse Core Ops, SparseCore 0:
  10.3 52.1 all-gather.4
  64.1 99.5 all-gather.2
  388.1 87.7 reduce-scatter.3
where the time goes:
time: 494 us; the launch traced here: 485 us
  matrix products  156 us (32%)
  waiting for transfers between devices  151 us (31%)
  local copies, waits for them, and re-layouts  98.8 us (20%)
  other arithmetic  40.3 us (8%)
  starting transfers between devices  23.8 us (5%)
  between operations  14.3 us (3%)
    all_gather x1, waiting for transfers between devices, per_device(): cot_all = lax.all_gather(out_grad, 'seq', axis=0, tiled=True)  83.5 us
    dot_general x25, matrix products, multiply(): return jnp.einsum(pattern, left, right, preferred_element_type=jnp.float32)  57.5 us
    dot_general x5, matrix products, tile_attention(): jnp.einsum('anb,antd->btd', owners, grad_key_near.reshape(tile_count, nei...  36.3 us
    dot_general x5, matrix products, tile_attention(): jnp.einsum('anb,antd->btd', owners, grad_value_near.reshape(tile_count, n...  25.7 us
    unnamed x56, local copies, waits for them, and re-layouts  24 us
    select_n x5, other arithmetic, tile_attention(): jnp.take(key_tiles, tile_pairs, axis=0)  20.2 us
    unnamed x4, waiting for transfers between devices  18 us
    all_to_all x1, waiting for transfers between devices, per_device(): lax.all_to_all(key_normed, 'seq', split_axis=1, concat_axis=0, tiled=True)  14.4 us
  transfers between devices with their start and end apart: 9, of which 8 were waited for; matrix products, arithmetic and copies ran while one was open for 12% of the time, Pallas kernels for 0%

commit v1 on v0

--- a/solution.py
+++ b/solution.py
@@ -6,6 +6,12 @@
 
 HEAD_DIM = 128
 EPS = 1e-06
+tiles_follow = lambda payload, axis_id, join_dim, at_axis: jnp.concatenate(
+    lax.all_to_all(
+        jnp.stack(jnp.split(payload, lax.axis_size(axis_id), axis=join_dim)), axis_id, 0, 0
+    ),
+    axis=at_axis,
+)
 
 
 def multiply(pattern, left, right):
@@ -81,7 +87,7 @@
     query_normed, query_scale = normalize(queries, gain_q)
     key_normed, key_scale = normalize(keys, gain_k)
     query_heads, key_heads, value_heads = (
-        lax.all_to_all(query_normed, "seq", split_axis=1, concat_axis=0, tiled=True),
+        tiles_follow(query_normed, "seq", 1, 0),
         lax.all_to_all(key_normed, "seq", split_axis=1, concat_axis=0, tiled=True),
         lax.all_to_all(values, "seq", split_axis=1, concat_axis=0, tiled=True),
     )

time: 494 us -> 494 us (level)
    reshape x4 -> x3, local copies, waits for them, and re-layouts: 10.8 us -> 9.36 us  [split(): field.reshape(tile_count, tile_rows, head_count, HEAD_DIM)]
  transfers between devices with their start and end apart: 9 -> 9, of which waited for: 8 -> 8; matrix products, arithmetic and copies ran while one was open for 12% -> 13% of each run, Pallas kernels for 0% -> 0%
where the time goes in v1:
time: 494 us; the launch traced here: 485 us
  matrix products  156 us (32%)
  waiting for transfers between devices  147 us (30%)
  local copies, waits for them, and re-layouts  101 us (20%)
  other arithmetic  41.6 us (8%)
  starting transfers between devices  23.8 us (5%)
  between operations  14.3 us (3%)
    all_gather x1, waiting for transfers between devices, per_device(): cot_all = lax.all_gather(out_grad, 'seq', axis=0, tiled=True)  83.6 us
    dot_general x25, matrix products, multiply(): return jnp.einsum(pattern, left, right, preferred_element_type=jnp.float32)  57.5 us
    dot_general x5, matrix products, tile_attention(): jnp.einsum('anb,antd->btd', owners, grad_key_near.reshape(tile_count, nei...  36.3 us
    dot_general x5, matrix products, tile_attention(): jnp.einsum('anb,antd->btd', owners, grad_value_near.reshape(tile_count, n...  25.7 us
    unnamed x56, local copies, waits for them, and re-layouts  24 us
    select_n x5, other arithmetic, tile_attention(): jnp.take(key_tiles, tile_pairs, axis=0)  20.1 us
    unnamed x4, waiting for transfers between devices  18 us
    all_to_all x1, waiting for transfers between devices, per_device(): lax.all_to_all(key_normed, 'seq', split_axis=1, concat_axis=0, tiled=True)  14.4 us
  transfers between devices with their start and end apart: 9, of which 8 were waited for; matrix products, arithmetic and copies ran while one was open for 13% of the time, Pallas kernels for 0%

profile of v1, /device:TPU:0, one launch (start us, length us, event | category | flops | bytes accessed | tf_op | source)
XLA Modules:
  0.0 484.8 jit_solution(10376774502786844932)
XLA Ops:
  12.1 4.5 all-to-all-start
  23.3 11.3 %all-to-all-done = bf16[4,256,640]{1,2,0:T(8,128)(2,1)S(1)} async-done(((bf16[4,256,640]{1,2,0:T(8,128)(2,1)}), bf16[4,256,640]{1,2,0:T(8,128)(2,1)S(1)}, u32[]{:S(2)}, u32[]{:S(2)}) %all-to-all-start) | async-done | bytes 1310752 | tf_op jit(solution)/shard_map/all_to_all | solution.py:10
  34.6 3.5 all-to-all-start.1
  40.6 14.4 %all-to-all-done.1 = bf16[256,4,640]{2,0,1:T(8,128)(2,1)S(1)} async-done(((bf16[256,4,640]{2,0,1:T(8,128)(2,1)}), bf16[256,4,640]{2,0,1:T(8,128)(2,1)S(1)}, u32[]{:S(2)}, u32[]{:S(2)}) %all-to-all-start.1) | async-done | bytes 1310752 | tf_op jit(solution)/shard_map/all_to_all | solution.py:91
  55.1 4.3 all-to-all-start.2
  62.6 3.1 reshape_reshape.3
  66.0 3.1 reshape.151
  70.5 5.0 %all-to-all-done.2 = bf16[256,4,640]{2,0,1:T(8,128)(2,1)} async-done(((bf16[256,4,640]{2,0,1:T(8,128)(2,1)}), bf16[256,4,640]{2,0,1:T(8,128)(2,1)}, u32[]{:S(2)}, u32[]{:S(2)}) %all-to-all-start.2) | async-done | bytes 1310752 | tf_op jit(solution)/shard_map/all_to_all | solution.py:92
  75.5 3.2 reshape.152
  80.1 83.6 %all-gather.3.cloned.1.call-done = bf16[1024,5120]{1,0:T(8,128)(2,1)} async-done(((bf16[256,5120]{1,0:T(8,128)(2,1)}), bf16[1024,5120]{1,0:T(8,128)(2,1)}) %all-gather.3.cloned.1.call-update) | async-done | bytes 10485776 | tf_op jit(solution)/shard_map/all_gather | solution.py:94
  163.8 13.8 %convolution_convert_fusion.1 = bf16[1024,640]{1,0:T(8,128)(2,1)} fusion(bf16[1024,5120]{1,0:T(8,128)(2,1)} %all-gather.3.cloned.1.call-done, bf16[5120,640]{1,0:T(8,128)(2,1)} %all-gather.5.cloned.1.call-done), kind=kOutput, calls=%fused_computation.95 | convolution fusion | flops 6711541760 | bytes 18350080 | tf_op jit(solution)/shard_map/dot_general | solution.py:96
  177.5 3.1 reshape.153
  182.1 182.5 %while.18 = (s32[]{:T(128)}, bf16[5,16,64,128]{3,2,1,0:T(8,128)(2,1)}, bf16[5,16,64,128]{3,2,1,0:T(8,128)(2,1)}, bf16[5,16,64,128]{3,1,2,0:T(8,128)(2,1)}, bf16[...) while((s32[]{:T(128)}, ...), condition=%wide.region_6.8_spmd, body=%wide.region_2.7_spmd.sunk | while | flops 1219638656 | bytes 88276472 | solution.py:109
  188.0 4.0 broadcast_select_fusion.6
  194.5 3.6 fusion.136
  204.6 7.3 %fusion.138 = bf16[5,16,64,128]{3,1,2,0:T(8,128)(2,1)} fusion(bf16[5,16,64,128]{3,1,2,0:T(8,128)(2,1)} %get-tuple-element.345, s32[]{:T(128)S(6)} %copy.142, f32[16,8,64,128]{3,2,1,0:T(8,128)} %bitcast.178, s32[16,8]{0,1:T(8,128)S(1)} %copy.132), kind=kOutput, calls=%fused_computation.26.clone.1 | convolution fusion | flops 201459712 | bytes 4456964 | tf_op jit(solution)/shard_map/while/body/eval_jaxpr/anb,antd->btd/dot_general | solution.py:61
  213.8 5.1 %fusion.140 = bf16[5,16,64,128]{3,1,2,0:T(8,128)(2,1)} fusion(bf16[5,16,64,128]{3,1,2,0:T(8,128)(2,1)} %get-tuple-element.346, s32[]{:T(128)S(6)} %copy.142, f32[16,8,64,128]{3,2,1,0:T(8,128)S(1)} %bitcast.183, s32[16,8]{0,1:T(8,128)S(1)} %copy.132), kind=kOutput, calls=%fused_computation.28.clone.1 | convolution fusion | flops 201459712 | bytes 4456964 | tf_op jit(solution)/shard_map/while/body/eval_jaxpr/anb,antd->btd/dot_general | solution.py:67
  224.3 4.0 broadcast_select_fusion.6
  230.9 3.6 fusion.136
  240.9 7.3 %fusion.138 = bf16[5,16,64,128]{3,1,2,0:T(8,128)(2,1)} fusion(bf16[5,16,64,128]{3,1,2,0:T(8,128)(2,1)} %get-tuple-element.345, s32[]{:T(128)S(6)} %copy.142, f32[16,8,64,128]{3,2,1,0:T(8,128)} %bitcast.178, s32[16,8]{0,1:T(8,128)S(1)} %copy.132), kind=kOutput, calls=%fused_computation.26.clone.1 | convolution fusion | flops 201459712 | bytes 4456964 | tf_op jit(solution)/shard_map/while/body/eval_jaxpr/anb,antd->btd/dot_general | solution.py:61
  250.1 5.1 %fusion.140 = bf16[5,16,64,128]{3,1,2,0:T(8,128)(2,1)} fusion(bf16[5,16,64,128]{3,1,2,0:T(8,128)(2,1)} %get-tuple-element.346, s32[]{:T(128)S(6)} %copy.142, f32[16,8,64,128]{3,2,1,0:T(8,128)S(1)} %bitcast.183, s32[16,8]{0,1:T(8,128)S(1)} %copy.132), kind=kOutput, calls=%fused_computation.28.clone.1 | convolution fusion | flops 201459712 | bytes 4456964 | tf_op jit(solution)/shard_map/while/body/eval_jaxpr/anb,antd->btd/dot_general | solution.py:67
  260.7 4.0 broadcast_select_fusion.6
  267.2 3.6 fusion.136
  274.4 2.8 convolution_multiply_fusion.3
  277.3 7.3 %fusion.138 = bf16[5,16,64,128]{3,1,2,0:T(8,128)(2,1)} fusion(bf16[5,16,64,128]{3,1,2,0:T(8,128)(2,1)} %get-tuple-element.345, s32[]{:T(128)S(6)} %copy.142, f32[16,8,64,128]{3,2,1,0:T(8,128)} %bitcast.178, s32[16,8]{0,1:T(8,128)S(1)} %copy.132), kind=kOutput, calls=%fused_computation.26.clone.1 | convolution fusion | flops 201459712 | bytes 4456964 | tf_op jit(solution)/shard_map/while/body/eval_jaxpr/anb,antd->btd/dot_general | solution.py:61
  286.5 5.1 %fusion.140 = bf16[5,16,64,128]{3,1,2,0:T(8,128)(2,1)} fusion(bf16[5,16,64,128]{3,1,2,0:T(8,128)(2,1)} %get-tuple-element.346, s32[]{:T(128)S(6)} %copy.142, f32[16,8,64,128]{3,2,1,0:T(8,128)S(1)} %bitcast.183, s32[16,8]{0,1:T(8,128)S(1)} %copy.132), kind=kOutput, calls=%fused_computation.28.clone.1 | convolution fusion | flops 201459712 | bytes 4456964 | tf_op jit(solution)/shard_map/while/body/eval_jaxpr/anb,antd->btd/dot_general | solution.py:67
  297.1 4.0 broadcast_select_fusion.6
  303.6 3.6 fusion.136
  310.8 2.8 convolution_multiply_fusion.3
  313.7 7.3 %fusion.138 = bf16[5,16,64,128]{3,1,2,0:T(8,128)(2,1)} fusion(bf16[5,16,64,128]{3,1,2,0:T(8,128)(2,1)} %get-tuple-element.345, s32[]{:T(128)S(6)} %copy.142, f32[16,8,64,128]{3,2,1,0:T(8,128)} %bitcast.178, s32[16,8]{0,1:T(8,128)S(1)} %copy.132), kind=kOutput, calls=%fused_computation.26.clone.1 | convolution fusion | flops 201459712 | bytes 4456964 | tf_op jit(solution)/shard_map/while/body/eval_jaxpr/anb,antd->btd/dot_general | solution.py:61
  322.9 5.2 %fusion.140 = bf16[5,16,64,128]{3,1,2,0:T(8,128)(2,1)} fusion(bf16[5,16,64,128]{3,1,2,0:T(8,128)(2,1)} %get-tuple-element.346, s32[]{:T(128)S(6)} %copy.142, f32[16,8,64,128]{3,2,1,0:T(8,128)S(1)} %bitcast.183, s32[16,8]{0,1:T(8,128)S(1)} %copy.132), kind=kOutput, calls=%fused_computation.28.clone.1 | convolution fusion | flops 201459712 | bytes 4456964 | tf_op jit(solution)/shard_map/while/body/eval_jaxpr/anb,antd->btd/dot_general | solution.py:67
  333.5 4.0 broadcast_select_fusion.6
  340.0 3.6 fusion.136
  350.1 7.3 %fusion.138 = bf16[5,16,64,128]{3,1,2,0:T(8,128)(2,1)} fusion(bf16[5,16,64,128]{3,1,2,0:T(8,128)(2,1)} %get-tuple-element.345, s32[]{:T(128)S(6)} %copy.142, f32[16,8,64,128]{3,2,1,0:T(8,128)} %bitcast.178, s32[16,8]{0,1:T(8,128)S(1)} %copy.132), kind=kOutput, calls=%fused_computation.26.clone.1 | convolution fusion | flops 201459712 | bytes 4456964 | tf_op jit(solution)/shard_map/while/body/eval_jaxpr/anb,antd->btd/dot_general | solution.py:61
  359.3 5.2 %fusion.140 = bf16[5,16,64,128]{3,1,2,0:T(8,128)(2,1)} fusion(bf16[5,16,64,128]{3,1,2,0:T(8,128)(2,1)} %get-tuple-element.346, s32[]{:T(128)S(6)} %copy.142, f32[16,8,64,128]{3,2,1,0:T(8,128)S(1)} %bitcast.183, s32[16,8]{0,1:T(8,128)S(1)} %copy.132), kind=kOutput, calls=%fused_computation.28.clone.1 | convolution fusion | flops 201459712 | bytes 4456964 | tf_op jit(solution)/shard_map/while/body/eval_jaxpr/anb,antd->btd/dot_general | solution.py:67
  367.0 11.5 %fusion.68 = bf16[5120,640]{0,1:T(8,128)(2,1)} fusion(bf16[1024,5120]{1,0:T(8,128)(2,1)} %all-gather.3.cloned.1.call-done, bf16[128,8,5,128]{3,2,1,0:T(8,128)(2,1)S(1)} %bitcast.195), kind=kOutput, calls=%fused_computation.66 | convolution fusion | flops 6717440000 | bytes 18350080 | tf_op jit(solution)/shard_map/td,te->de/dot_general | solution.py:119
  378.5 9.5 %copy.97 = bf16[5120,640]{1,0:T(8,128)(2,1)} copy(bf16[5120,640]{0,1:T(8,128)(2,1)} %fusion.68) | data formatting | bytes 13107200
  392.8 4.0 all-to-all-start.3
  406.3 8.4 %all-to-all-done.3 = bf16[4,256,640]{2,1,0:T(8,128)(2,1)S(1)} async-done(((bf16[4,256,640]{2,1,0:T(8,128)(2,1)}), bf16[4,256,640]{2,1,0:T(8,128)(2,1)S(1)}, u32[]{:S(2)}, u32[]{:S(2)}) %all-to-all-start.3) | async-done | bytes 1310752 | tf_op jit(solution)/shard_map/all_to_all | solution.py:127
  415.8 3.8 all-to-all-start.4
  419.5 3.1 convert_bitcast_fusion.1
  422.6 3.4 copy.85
  432.7 3.7 all-to-all-done.4
  437.5 3.5 all-to-all-start.5
  441.1 3.0 convert_bitcast_fusion
  444.0 3.4 copy.87
  454.2 2.9 all-to-all-done.5
  459.4 16.6 %reduce-scatter.4.cloned.1.call-done = bf16[160,640]{1,0:T(8,128)(2,1)} async-done(((bf16[5120,640]{1,0:T(8,128)(2,1)}), bf16[160,640]{1,0:T(8,128)(2,1)}) %reduce-scatter.4.cloned.1.call-update) | async-done | bytes 204816
  (218 shorter events, 133.9 us)
Async XLA Ops:
  7.2 52.6 %copy-start = (s32[1,16]{1,0:T(1,128)S(1)}, s32[1,16]{1,0:T(1,128)}, u32[]{:S(2)}) copy-start(s32[1,16]{1,0:T(1,128)} %param.19) | copy-start | bytes 196
  7.2 1.5 copy-start.14
  7.2 72.9 %all-gather.5.cloned.1.call-start = ((), (), s32[]{:S(2)}) async-start(), calls=%async_computation.8 | async-start | bytes 6758400 | tf_op jit(solution)/shard_map/all_gather | solution.py:97
  7.9 155.8 %all-gather.3.cloned.1.call-start = ((), (), s32[]{:S(2)}) async-start(), calls=%async_computation.7 | async-start | bytes 13107200 | tf_op jit(solution)/shard_map/all_gather | solution.py:94
  8.7 1.6 copy-start.16
  9.3 1.5 copy-start.5
  10.3 0.6 copy-start.21
  12.1 22.5 %all-to-all-start = ((bf16[4,256,640]{1,2,0:T(8,128)(2,1)}), bf16[4,256,640]{1,2,0:T(8,128)(2,1)S(1)}, u32[]{:S(2)}, u32[]{:S(2)}) async-start(bf16[4,256,640]{1,2,0:T(8,128)(2,1)} %pad_maximum_fusion), calls=%async_computation | async-start | bytes 2621440 | tf_op jit(solution)/shard_map/all_to_all | solution.py:10
  16.7 2.7 copy-start.18
  18.3 5.0 %copy-start.7 = (bf16[256,2560]{0,1:T(8,128)(2,1)}, bf16[256,2560]{0,1:T(8,128)(2,1)S(1)}, u32[]{:S(2)}) copy-start(bf16[256,2560]{0,1:T(8,128)(2,1)S(1)} %copy.74) | copy-start | bytes 3932164
  19.4 1.5 copy-start.23
  34.6 20.5 %all-to-all-start.1 = ((bf16[256,4,640]{2,0,1:T(8,128)(2,1)}), bf16[256,4,640]{2,0,1:T(8,128)(2,1)S(1)}, u32[]{:S(2)}, u32[]{:S(2)}) async-start(bf16[256,4,640]{2,0,1:T(8,128)(2,1)} %copy.75), calls=%async_computation.1 | async-start | bytes 2621440 | tf_op jit(solution)/shard_map/all_to_all | solution.py:91
  38.1 21.4 %copy-start.20 = (s32[16,8]{0,1:T(8,128)S(1)}, s32[16,8]{0,1:T(8,128)}, u32[]{:S(2)}) copy-start(s32[16,8]{0,1:T(8,128)} %param.18) | copy-start | bytes 1540
  55.1 5.9 %copy-start.11 = (bf16[256,4,640]{2,0,1:T(8,128)(2,1)}, bf16[256,4,640]{2,0,1:T(8,128)(2,1)S(1)}, u32[]{:S(2)}) copy-start(bf16[256,4,640]{2,0,1:T(8,128)(2,1)S(1)} %all-to-all-done.1) | copy-start | bytes 3932164
  55.1 20.5 %all-to-all-start.2 = ((bf16[256,4,640]{2,0,1:T(8,128)(2,1)}), bf16[256,4,640]{2,0,1:T(8,128)(2,1)}, u32[]{:S(2)}, u32[]{:S(2)}) async-start(bf16[256,4,640]{2,0,1:T(8,128)(2,1)} %bitcast.191), calls=%async_computation.2 | async-start | bytes 2621440 | tf_op jit(solution)/shard_map/all_to_all | solution.py:92
  59.4 416.6 %reduce-scatter.4.cloned.1.call-start = ((), (), s32[]{:S(2)}) async-start(), calls=%async_computation.9 | async-start | bytes 6758400
  194.5 3.6 copy-start.2
  194.5 3.6 copy-start.3
  204.6 7.3 %copy-start.4 = (f32[16,64,512]{2,1,0:T(8,128)S(1)}, f32[16,64,512]{2,1,0:T(8,128)}, u32[]{:S(2)}) copy-start(f32[16,64,512]{2,1,0:T(8,128)} %get-tuple-element.326) | copy-start | bytes 6291460 | tf_op jit(solution)/shard_map/while
  230.9 3.6 copy-start.2
  230.9 3.6 copy-start.3
  240.9 7.3 %copy-start.4 = (f32[16,64,512]{2,1,0:T(8,128)S(1)}, f32[16,64,512]{2,1,0:T(8,128)}, u32[]{:S(2)}) copy-start(f32[16,64,512]{2,1,0:T(8,128)} %get-tuple-element.326) | copy-start | bytes 6291460 | tf_op jit(solution)/shard_map/while
  267.2 3.6 copy-start.2
  267.2 3.6 copy-start.3
  277.3 7.3 %copy-start.4 = (f32[16,64,512]{2,1,0:T(8,128)S(1)}, f32[16,64,512]{2,1,0:T(8,128)}, u32[]{:S(2)}) copy-start(f32[16,64,512]{2,1,0:T(8,128)} %get-tuple-element.326) | copy-start | bytes 6291460 | tf_op jit(solution)/shard_map/while
  303.6 3.6 copy-start.2
  303.6 3.6 copy-start.3
  313.7 7.3 %copy-start.4 = (f32[16,64,512]{2,1,0:T(8,128)S(1)}, f32[16,64,512]{2,1,0:T(8,128)}, u32[]{:S(2)}) copy-start(f32[16,64,512]{2,1,0:T(8,128)} %get-tuple-element.326) | copy-start | bytes 6291460 | tf_op jit(solution)/shard_map/while
  340.0 3.6 copy-start.2
  340.0 3.6 copy-start.3
  350.1 7.3 %copy-start.4 = (f32[16,64,512]{2,1,0:T(8,128)S(1)}, f32[16,64,512]{2,1,0:T(8,128)}, u32[]{:S(2)}) copy-start(f32[16,64,512]{2,1,0:T(8,128)} %get-tuple-element.326) | copy-start | bytes 6291460 | tf_op jit(solution)/shard_map/while
  388.0 1.3 copy-start.15
  392.8 21.9 %all-to-all-start.3 = ((bf16[4,256,640]{2,1,0:T(8,128)(2,1)}), bf16[4,256,640]{2,1,0:T(8,128)(2,1)S(1)}, u32[]{:S(2)}, u32[]{:S(2)}) async-start(bf16[4,256,640]{2,1,0:T(8,128)(2,1)} %all_to_all.68), calls=%async_computation.3 | async-start | bytes 2621440 | tf_op jit(solution)/shard_map/all_to_all | solution.py:127
  414.7 1.1 copy-start.13
  415.8 20.7 %all-to-all-start.4 = ((bf16[4,256,640]{2,1,0:T(8,128)(2,1)}), bf16[4,256,640]{2,1,0:T(8,128)(2,1)S(1)}, u32[]{:S(2)}, u32[]{:S(2)}) async-start(bf16[4,256,640]{2,1,0:T(8,128)(2,1)} %all_to_all.70), calls=%async_computation.4 | async-start | bytes 2621440 | tf_op jit(solution)/shard_map/all_to_all | solution.py:128
  422.6 3.4 copy-start.6
  422.6 3.4 copy-start.17
  426.0 2.5 copy-start.9
  426.0 2.5 copy-start.22
  426.0 2.5 copy-start.25
  436.5 1.1 copy-start.12
  437.5 19.6 %all-to-all-start.5 = ((bf16[4,256,640]{2,1,0:T(8,128)(2,1)}), bf16[4,256,640]{2,1,0:T(8,128)(2,1)S(1)}, u32[]{:S(2)}, u32[]{:S(2)}) async-start(bf16[4,256,640]{2,1,0:T(8,128)(2,1)} %all_to_all.72), calls=%async_computation.5 | async-start | bytes 2621440 | tf_op jit(solution)/shard_map/all_to_all | solution.py:129
  444.0 3.4 copy-start.8
  444.0 3.4 copy-start.19
  447.5 2.6 copy-start.10
  447.5 2.6 copy-start.24
  447.5 2.6 copy-start.26
  457.1 20.9 %copy-start.1 = (s32[1,16]{1,0:T(1,128)S(1)}, s32[1,16]{1,0:T(1,128)}, u32[]{:S(2)}) copy-start(s32[1,16]{1,0:T(1,128)} %param.19) | copy-start | bytes 196
Sparse Core Ops, SparseCore 0:
  10.3 52.1 all-gather.4
  64.1 99.5 all-gather.2
  388.2 87.7 reduce-scatter.3
